TPU v7x, 128 devices: a whole 4x4x4 slice. The times are simulated.
128 devices in a mesh: pipe: 8 (over y, core), tensor: 16 (over x, z).
Axes of the slice: x: 4, y: 4, z: 4, core: 2. Of those that a mesh axis runs over, the one named last changes fastest.
Arguments:
- inputs: bfloat16 [128, 4096], P(None, 'tensor'), may hold values from -6 to 6
- out_grad: bfloat16 [128, 4096], P(None, 'tensor'), may hold values from -6 to 6
- norm_gain: float32 [8, 4096], P('pipe'), may hold values from 0.25 to 1.75
- gate_weight: bfloat16 [8, 4096, 14336], P('pipe', None, 'tensor'), may hold values from -0.125 to 0.125
- up_weight: bfloat16 [8, 4096, 14336], P('pipe', None, 'tensor'), may hold values from -0.125 to 0.125
- down_weight: bfloat16 [8, 14336, 4096], P('pipe', 'tensor'), may hold values from -0.0625 to 0.0625
- block_mask: int32 [8, 3, 32, 112], P('pipe', None, None, 'tensor'), may hold values from 0 to 1, as said below
Outputs:
- section_out: float32 [8, 128, 4096], P('pipe')
- section_grad: float32 [8, 128, 4096], P('pipe')
Inputs may be any that keep to these rules, and one draw needn't show every extreme that they name: `block_mask`: 1 keeps a block, 0 drops it; the share kept differs from one block column to another.
All inputs are finite; a program needn't handle non-finite values.
Results may differ from a plain program's by a relative error of at most 0.02.
Values may be sent and summed in bfloat16 or wider, within the bound.
A program may use at most 128 MiB of HBM per device.

v0:
```python
import jax
import jax.numpy as jnp
from jax import lax
from jax.sharding import PartitionSpec as P

BLOCK = 128
ROWS = 64


def shifted(value, axis, steps):
    count = lax.axis_size(axis)
    first, last = (max(0, -steps), min(count, count - steps))
    return lax.ppermute(value, axis, [(source, source + steps) for source in range(first, last)])


def masked_blocks(weight, mask):
    rows, cols = weight.shape
    shaped = weight.reshape(rows // BLOCK, BLOCK, cols // BLOCK, BLOCK)
    return (shaped * mask.astype(weight.dtype)[:, None, :, None]).reshape(rows, cols)


def contract_last(left, right):
    return lax.dot_general(
        left, right, (((1,), (1,)), ((), ())), preferred_element_type=jnp.float32
    )


def norm_back(xval, avec, scale):
    inner = jnp.mean(avec * xval, axis=-1, keepdims=True)
    return scale * avec - xval * scale * scale * scale * inner


def retain_place(buffer, value, store_place, valid_flag):
    older = lax.dynamic_index_in_dim(buffer, store_place, 0, keepdims=False)
    return lax.dynamic_update_index_in_dim(
        buffer, jnp.where(valid_flag, value, older), store_place, 0
    )


def local(inputs, out_grad, norm_gain, gate_weight, up_weight, down_weight, block_mask):
    eps = 1e-05
    whole_in, whole_grad = (
        lax.all_gather(inputs, "tensor", axis=1, tiled=True),
        lax.all_gather(out_grad, "tensor", axis=1, tiled=True),
    )
    width = whole_in.shape[1]
    count = whole_in.shape[0] // ROWS
    whole_in = whole_in.reshape(count, ROWS, width)
    whole_grad = whole_grad.reshape(count, ROWS, width)
    gmat = masked_blocks(gate_weight[0], block_mask[0, 0])
    umat = masked_blocks(up_weight[0], block_mask[0, 1])
    dmat = masked_blocks(down_weight[0], block_mask[0, 2].T)
    gain = norm_gain[0]
    hidden_cols = gmat.shape[1]
    section = lax.axis_index("pipe")
    sections = lax.axis_size("pipe")
    step_total = count + sections - 1
    sent_rows = ROWS

    def forward_step_once(tick, loop_state):
        arriving_rows, input_store, gate_store, upper_store, output_store = loop_state
        micro = tick - section
        valid_flag = (micro >= 0) & (micro < count)
        store_place = jnp.clip(micro, 0, count - 1)
        first = lax.dynamic_index_in_dim(whole_in, store_place, 0, keepdims=False).astype(
            jnp.float32
        )
        xval = jnp.where(section == 0, first, arriving_rows)
        scale = lax.rsqrt(jnp.mean(xval * xval, axis=-1, keepdims=True) + eps)
        normed = (xval * scale * gain).astype(jnp.bfloat16)
        gate_matrix = jnp.dot(normed, gmat, preferred_element_type=jnp.float32)
        upval = jnp.dot(normed, umat, preferred_element_type=jnp.float32)
        hidden = (jax.nn.silu(gate_matrix) * upval).astype(jnp.bfloat16)
        partial_out = jnp.dot(hidden, dmat, preferred_element_type=jnp.float32)
        summed = lax.psum(partial_out, "tensor")
        result = xval + summed
        input_store = retain_place(input_store, xval, store_place, valid_flag)
        gate_store = retain_place(gate_store, gate_matrix, store_place, valid_flag)
        upper_store = retain_place(upper_store, upval, store_place, valid_flag)
        output_store = retain_place(output_store, result, store_place, valid_flag)
        handed_rows = shifted(result, "pipe", 1)
        return (handed_rows, input_store, gate_store, upper_store, output_store)

    first_position = (
        jnp.zeros((sent_rows, width), jnp.float32),
        jnp.zeros((count, ROWS, width), jnp.float32),
        jnp.zeros((count, ROWS, hidden_cols), jnp.float32),
        jnp.zeros((count, ROWS, hidden_cols), jnp.float32),
        jnp.zeros((count, sent_rows, width), jnp.float32),
    )
    unused_value, input_store, gate_store, upper_store, output_store = lax.fori_loop(
        0, step_total, forward_step_once, first_position
    )

    def backward_tick(tick, loop_state):
        arriving_rows, dbuf = loop_state
        micro = tick - (sections - 1 - section)
        valid_flag = (micro >= 0) & (micro < count)
        store_place = jnp.clip(micro, 0, count - 1)
        last = lax.dynamic_index_in_dim(whole_grad, store_place, 0, keepdims=False).astype(
            jnp.float32
        )
        cot = jnp.where(section == sections - 1, last, arriving_rows)
        xval = lax.dynamic_index_in_dim(input_store, store_place, 0, keepdims=False)
        gate_matrix = lax.dynamic_index_in_dim(gate_store, store_place, 0, keepdims=False)
        upval = lax.dynamic_index_in_dim(upper_store, store_place, 0, keepdims=False)
        dhid = contract_last(cot.astype(jnp.bfloat16), dmat)
        sig = jax.nn.sigmoid(gate_matrix)
        dgate = (dhid * upval * sig * (1.0 + gate_matrix * (1.0 - sig))).astype(jnp.bfloat16)
        dup = (dhid * gate_matrix * sig).astype(jnp.bfloat16)
        partial_grad = contract_last(dgate, gmat) + contract_last(dup, umat)
        dnorm = lax.psum(partial_grad, "tensor")
        scale = lax.rsqrt(jnp.mean(xval * xval, axis=-1, keepdims=True) + eps)
        result = cot + norm_back(xval, dnorm * gain, scale)
        dbuf = retain_place(dbuf, result, store_place, valid_flag)
        handed_rows = shifted(result, "pipe", -1)
        return (handed_rows, dbuf)

    begin = (
        jnp.zeros((sent_rows, width), jnp.float32),
        jnp.zeros((count, sent_rows, width), jnp.float32),
    )
    unused_value, dbuf = lax.fori_loop(0, step_total, backward_tick, begin)
    return (output_store.reshape(1, count * ROWS, width), dbuf.reshape(1, count * ROWS, width))


def solution(mesh):
    in_specs = (
        P(None, "tensor"),
        P(None, "tensor"),
        P("pipe", None),
        P("pipe", None, "tensor"),
        P("pipe", None, "tensor"),
        P("pipe", "tensor", None),
        P("pipe", None, None, "tensor"),
    )
    out_specs = (P("pipe", None, None), P("pipe", None, None))
    return jax.shard_map(local, mesh=mesh, in_specs=in_specs, out_specs=out_specs, check_vma=False)
```

profile of v0, /device:TPU:0, one launch (start us, length us, event | category | flops | bytes accessed | tf_op | source)
XLA Modules:
  0.0 2317.8 jit_solution(494138706350829965)
XLA Ops:
  8.6 10.7 copy.12
  19.3 10.7 copy.11
  30.1 3.9 mul.305
  34.0 10.6 bitcast_multiply_fusion.7
  48.5 10.6 bitcast_multiply_fusion.8
  59.1 10.8 copy.14
  69.9 10.7 copy.13
  80.6 4.0 mul.308
  84.6 10.6 bitcast_multiply_fusion.6
  99.9 1091.6 %while.39 = (s32[]{:T(128)}, f32[64,4096]{1,0:T(8,128)S(1)}, f32[2,64,4096]{2,1,0:T(8,128)}, f32[2,64,896]{2,1,0:T(8,128)}, f32[2,64,896]{2,1,0:T(8,128)}, /*ind...) while((s32[]{:T(128)}, f32[64,4096]{1,0:T(8,128)S(1)}, ...), condition=%wide.region_3.4_spmd, body=%wide.region_0.3_spmd.sunk | while | flops 1413677056 | bytes 128075888 | solution.py:91
  105.6 5.3 bitcast_dynamic-update-slice_fusion.9
  118.1 87.3 %all-reduce.3.cloned.1.call-done = f32[64,4096]{1,0:T(8,128)} async-done(((f32[64,4096]{1,0:T(8,128)}), f32[64,4096]{1,0:T(8,128)}) %all-reduce.3.cloned.1.call-update) | async-done | bytes 1048592 | tf_op jit(solution)/shard_map/while/body/eval_jaxpr/psum | solution.py:75
  218.6 5.3 bitcast_dynamic-update-slice_fusion.9
  231.1 96.6 %all-reduce.3.cloned.1.call-done = f32[64,4096]{1,0:T(8,128)} async-done(((f32[64,4096]{1,0:T(8,128)}), f32[64,4096]{1,0:T(8,128)}) %all-reduce.3.cloned.1.call-update) | async-done | bytes 1048592 | tf_op jit(solution)/shard_map/while/body/eval_jaxpr/psum | solution.py:75
  340.9 5.3 bitcast_dynamic-update-slice_fusion.9
  353.4 96.6 %all-reduce.3.cloned.1.call-done = f32[64,4096]{1,0:T(8,128)} async-done(((f32[64,4096]{1,0:T(8,128)}), f32[64,4096]{1,0:T(8,128)}) %all-reduce.3.cloned.1.call-update) | async-done | bytes 1048592 | tf_op jit(solution)/shard_map/while/body/eval_jaxpr/psum | solution.py:75
  463.2 5.3 bitcast_dynamic-update-slice_fusion.9
  475.8 96.7 %all-reduce.3.cloned.1.call-done = f32[64,4096]{1,0:T(8,128)} async-done(((f32[64,4096]{1,0:T(8,128)}), f32[64,4096]{1,0:T(8,128)}) %all-reduce.3.cloned.1.call-update) | async-done | bytes 1048592 | tf_op jit(solution)/shard_map/while/body/eval_jaxpr/psum | solution.py:75
  585.6 5.3 bitcast_dynamic-update-slice_fusion.9
  598.1 96.7 %all-reduce.3.cloned.1.call-done = f32[64,4096]{1,0:T(8,128)} async-done(((f32[64,4096]{1,0:T(8,128)}), f32[64,4096]{1,0:T(8,128)}) %all-reduce.3.cloned.1.call-update) | async-done | bytes 1048592 | tf_op jit(solution)/shard_map/while/body/eval_jaxpr/psum | solution.py:75
  708.0 5.3 bitcast_dynamic-update-slice_fusion.9
  720.5 96.6 %all-reduce.3.cloned.1.call-done = f32[64,4096]{1,0:T(8,128)} async-done(((f32[64,4096]{1,0:T(8,128)}), f32[64,4096]{1,0:T(8,128)}) %all-reduce.3.cloned.1.call-update) | async-done | bytes 1048592 | tf_op jit(solution)/shard_map/while/body/eval_jaxpr/psum | solution.py:75
  830.3 5.3 bitcast_dynamic-update-slice_fusion.9
  842.8 96.6 %all-reduce.3.cloned.1.call-done = f32[64,4096]{1,0:T(8,128)} async-done(((f32[64,4096]{1,0:T(8,128)}), f32[64,4096]{1,0:T(8,128)}) %all-reduce.3.cloned.1.call-update) | async-done | bytes 1048592 | tf_op jit(solution)/shard_map/while/body/eval_jaxpr/psum | solution.py:75
  952.6 5.3 bitcast_dynamic-update-slice_fusion.9
  965.1 96.7 %all-reduce.3.cloned.1.call-done = f32[64,4096]{1,0:T(8,128)} async-done(((f32[64,4096]{1,0:T(8,128)}), f32[64,4096]{1,0:T(8,128)}) %all-reduce.3.cloned.1.call-update) | async-done | bytes 1048592 | tf_op jit(solution)/shard_map/while/body/eval_jaxpr/psum | solution.py:75
  1074.9 5.3 bitcast_dynamic-update-slice_fusion.9
  1087.5 96.6 %all-reduce.3.cloned.1.call-done = f32[64,4096]{1,0:T(8,128)} async-done(((f32[64,4096]{1,0:T(8,128)}), f32[64,4096]{1,0:T(8,128)}) %all-reduce.3.cloned.1.call-update) | async-done | bytes 1048592 | tf_op jit(solution)/shard_map/while/body/eval_jaxpr/psum | solution.py:75
  1192.3 57.3 %all-gather.5.cloned.1.call-done = bf16[128,4096]{1,0:T(8,128)(2,1)} async-done(((bf16[128,256]{1,0:T(8,128)(2,1)}), bf16[128,4096]{1,0:T(8,128)(2,1)}) %all-gather.5.cloned.1.call-update) | async-done | bytes 1048592 | tf_op jit(solution)/shard_map/all_gather | solution.py:44
  1251.2 1059.8 %while.40 = (s32[]{:T(128)}, f32[64,4096]{1,0:T(8,128)S(1)}, f32[2,64,4096]{2,1,0:T(8,128)}, pred[]{:T(512)}, s32[]{:T(128)}, /*index=5*/bf16[2,64,4096]{2,1,0:T...) while((s32[]{:T(128)}, f32[64,4096]{1,0:T(8,128)S(1)}, ...), condition=%wide.region_8.9_spmd, body=%wide.region_4.8_spmd.sunk | while | flops 1415446528 | bytes 114920952 | solution.py:123
  1251.5 5.7 fusion.74
  1265.4 84.5 %all-reduce.5.cloned.1.call-done = f32[64,4096]{1,0:T(8,128)} async-done(((f32[64,4096]{1,0:T(8,128)}), f32[64,4096]{1,0:T(8,128)}) %all-reduce.5.cloned.1.call-update) | async-done | bytes 1048592 | tf_op jit(solution)/shard_map/while/body/eval_jaxpr/psum | solution.py:112
  1359.6 5.8 fusion.74
  1373.5 95.3 %all-reduce.5.cloned.1.call-done = f32[64,4096]{1,0:T(8,128)} async-done(((f32[64,4096]{1,0:T(8,128)}), f32[64,4096]{1,0:T(8,128)}) %all-reduce.5.cloned.1.call-update) | async-done | bytes 1048592 | tf_op jit(solution)/shard_map/while/body/eval_jaxpr/psum | solution.py:112
  1478.5 5.7 fusion.74
  1492.4 95.3 %all-reduce.5.cloned.1.call-done = f32[64,4096]{1,0:T(8,128)} async-done(((f32[64,4096]{1,0:T(8,128)}), f32[64,4096]{1,0:T(8,128)}) %all-reduce.5.cloned.1.call-update) | async-done | bytes 1048592 | tf_op jit(solution)/shard_map/while/body/eval_jaxpr/psum | solution.py:112
  1597.5 5.7 fusion.74
  1611.3 95.3 %all-reduce.5.cloned.1.call-done = f32[64,4096]{1,0:T(8,128)} async-done(((f32[64,4096]{1,0:T(8,128)}), f32[64,4096]{1,0:T(8,128)}) %all-reduce.5.cloned.1.call-update) | async-done | bytes 1048592 | tf_op jit(solution)/shard_map/while/body/eval_jaxpr/psum | solution.py:112
  1716.4 5.7 fusion.74
  1730.2 95.3 %all-reduce.5.cloned.1.call-done = f32[64,4096]{1,0:T(8,128)} async-done(((f32[64,4096]{1,0:T(8,128)}), f32[64,4096]{1,0:T(8,128)}) %all-reduce.5.cloned.1.call-update) | async-done | bytes 1048592 | tf_op jit(solution)/shard_map/while/body/eval_jaxpr/psum | solution.py:112
  1835.3 5.7 fusion.74
  1849.2 95.3 %all-reduce.5.cloned.1.call-done = f32[64,4096]{1,0:T(8,128)} async-done(((f32[64,4096]{1,0:T(8,128)}), f32[64,4096]{1,0:T(8,128)}) %all-reduce.5.cloned.1.call-update) | async-done | bytes 1048592 | tf_op jit(solution)/shard_map/while/body/eval_jaxpr/psum | solution.py:112
  1954.3 5.7 fusion.74
  1968.1 95.3 %all-reduce.5.cloned.1.call-done = f32[64,4096]{1,0:T(8,128)} async-done(((f32[64,4096]{1,0:T(8,128)}), f32[64,4096]{1,0:T(8,128)}) %all-reduce.5.cloned.1.call-update) | async-done | bytes 1048592 | tf_op jit(solution)/shard_map/while/body/eval_jaxpr/psum | solution.py:112
  2073.2 5.7 fusion.74
  2087.0 95.3 %all-reduce.5.cloned.1.call-done = f32[64,4096]{1,0:T(8,128)} async-done(((f32[64,4096]{1,0:T(8,128)}), f32[64,4096]{1,0:T(8,128)}) %all-reduce.5.cloned.1.call-update) | async-done | bytes 1048592 | tf_op jit(solution)/shard_map/while/body/eval_jaxpr/psum | solution.py:112
  2192.1 5.7 fusion.74
  2206.0 95.3 %all-reduce.5.cloned.1.call-done = f32[64,4096]{1,0:T(8,128)} async-done(((f32[64,4096]{1,0:T(8,128)}), f32[64,4096]{1,0:T(8,128)}) %all-reduce.5.cloned.1.call-update) | async-done | bytes 1048592 | tf_op jit(solution)/shard_map/while/body/eval_jaxpr/psum | solution.py:112
  (568 shorter events, 354.8 us)
Async XLA Ops:
  7.2 88.0 %all-gather.3.cloned.1.call-start = ((), (), s32[]{:S(2)}) async-start(), calls=%async_computation | async-start | bytes 1114112 | tf_op jit(solution)/shard_map/all_gather | solution.py:43
  99.9 105.5 %all-reduce.3.cloned.1.call-start = ((), (), s32[]{:S(2)}) async-start(), calls=%async_computation.2 | async-start | bytes 2097152 | tf_op jit(solution)/shard_map/while/body/eval_jaxpr/psum | solution.py:75
  209.2 3.8 collective-permute-start
  213.0 114.8 %all-reduce.3.cloned.1.call-start = ((), (), s32[]{:S(2)}) async-start(), calls=%async_computation.2 | async-start | bytes 2097152 | tf_op jit(solution)/shard_map/while/body/eval_jaxpr/psum | solution.py:75
  226.0 101.8 %copy-start.3 = (f32[64,4096]{1,0:T(8,128)S(1)}, f32[64,4096]{1,0:T(8,128)}, u32[]{:S(2)}) copy-start(f32[64,4096]{1,0:T(8,128)} %copy-done.2) | copy-start | bytes 3145732 | tf_op jit(solution)/shard_map/while
  331.5 3.8 collective-permute-start
  335.3 114.8 %all-reduce.3.cloned.1.call-start = ((), (), s32[]{:S(2)}) async-start(), calls=%async_computation.2 | async-start | bytes 2097152 | tf_op jit(solution)/shard_map/while/body/eval_jaxpr/psum | solution.py:75
  348.3 101.8 %copy-start.3 = (f32[64,4096]{1,0:T(8,128)S(1)}, f32[64,4096]{1,0:T(8,128)}, u32[]{:S(2)}) copy-start(f32[64,4096]{1,0:T(8,128)} %copy-done.2) | copy-start | bytes 3145732 | tf_op jit(solution)/shard_map/while
  453.8 3.8 collective-permute-start
  457.6 114.8 %all-reduce.3.cloned.1.call-start = ((), (), s32[]{:S(2)}) async-start(), calls=%async_computation.2 | async-start | bytes 2097152 | tf_op jit(solution)/shard_map/while/body/eval_jaxpr/psum | solution.py:75
  470.6 101.8 %copy-start.3 = (f32[64,4096]{1,0:T(8,128)S(1)}, f32[64,4096]{1,0:T(8,128)}, u32[]{:S(2)}) copy-start(f32[64,4096]{1,0:T(8,128)} %copy-done.2) | copy-start | bytes 3145732 | tf_op jit(solution)/shard_map/while
  576.2 3.8 collective-permute-start
  579.9 114.9 %all-reduce.3.cloned.1.call-start = ((), (), s32[]{:S(2)}) async-start(), calls=%async_computation.2 | async-start | bytes 2097152 | tf_op jit(solution)/shard_map/while/body/eval_jaxpr/psum | solution.py:75
  593.0 101.9 %copy-start.3 = (f32[64,4096]{1,0:T(8,128)S(1)}, f32[64,4096]{1,0:T(8,128)}, u32[]{:S(2)}) copy-start(f32[64,4096]{1,0:T(8,128)} %copy-done.2) | copy-start | bytes 3145732 | tf_op jit(solution)/shard_map/while
  698.6 3.8 collective-permute-start
  702.3 114.8 %all-reduce.3.cloned.1.call-start = ((), (), s32[]{:S(2)}) async-start(), calls=%async_computation.2 | async-start | bytes 2097152 | tf_op jit(solution)/shard_map/while/body/eval_jaxpr/psum | solution.py:75
  715.3 101.8 %copy-start.3 = (f32[64,4096]{1,0:T(8,128)S(1)}, f32[64,4096]{1,0:T(8,128)}, u32[]{:S(2)}) copy-start(f32[64,4096]{1,0:T(8,128)} %copy-done.2) | copy-start | bytes 3145732 | tf_op jit(solution)/shard_map/while
  820.9 3.8 collective-permute-start
  824.7 114.8 %all-reduce.3.cloned.1.call-start = ((), (), s32[]{:S(2)}) async-start(), calls=%async_computation.2 | async-start | bytes 2097152 | tf_op jit(solution)/shard_map/while/body/eval_jaxpr/psum | solution.py:75
  837.7 101.8 %copy-start.3 = (f32[64,4096]{1,0:T(8,128)S(1)}, f32[64,4096]{1,0:T(8,128)}, u32[]{:S(2)}) copy-start(f32[64,4096]{1,0:T(8,128)} %copy-done.2) | copy-start | bytes 3145732 | tf_op jit(solution)/shard_map/while
  943.2 3.8 collective-permute-start
  946.9 114.8 %all-reduce.3.cloned.1.call-start = ((), (), s32[]{:S(2)}) async-start(), calls=%async_computation.2 | async-start | bytes 2097152 | tf_op jit(solution)/shard_map/while/body/eval_jaxpr/psum | solution.py:75
  960.0 101.8 %copy-start.3 = (f32[64,4096]{1,0:T(8,128)S(1)}, f32[64,4096]{1,0:T(8,128)}, u32[]{:S(2)}) copy-start(f32[64,4096]{1,0:T(8,128)} %copy-done.2) | copy-start | bytes 3145732 | tf_op jit(solution)/shard_map/while
  1065.5 3.8 collective-permute-start
  1069.3 114.8 %all-reduce.3.cloned.1.call-start = ((), (), s32[]{:S(2)}) async-start(), calls=%async_computation.2 | async-start | bytes 2097152 | tf_op jit(solution)/shard_map/while/body/eval_jaxpr/psum | solution.py:75
  1082.3 101.8 %copy-start.3 = (f32[64,4096]{1,0:T(8,128)S(1)}, f32[64,4096]{1,0:T(8,128)}, u32[]{:S(2)}) copy-start(f32[64,4096]{1,0:T(8,128)} %copy-done.2) | copy-start | bytes 3145732 | tf_op jit(solution)/shard_map/while
  1187.8 3.8 collective-permute-start
  1191.6 58.0 %all-gather.5.cloned.1.call-start = ((), (), s32[]{:S(2)}) async-start(), calls=%async_computation.1 | async-start | bytes 1114112 | tf_op jit(solution)/shard_map/all_gather | solution.py:44
  1251.4 98.5 %all-reduce.5.cloned.1.call-start = ((), (), s32[]{:S(2)}) async-start(), calls=%async_computation.3 | async-start | bytes 2097152 | tf_op jit(solution)/shard_map/while/body/eval_jaxpr/psum | solution.py:112
  1354.8 4.8 collective-permute-start.1
  1359.6 109.2 %all-reduce.5.cloned.1.call-start = ((), (), s32[]{:S(2)}) async-start(), calls=%async_computation.3 | async-start | bytes 2097152 | tf_op jit(solution)/shard_map/while/body/eval_jaxpr/psum | solution.py:112
  1473.7 4.8 collective-permute-start.1
  1478.5 109.2 %all-reduce.5.cloned.1.call-start = ((), (), s32[]{:S(2)}) async-start(), calls=%async_computation.3 | async-start | bytes 2097152 | tf_op jit(solution)/shard_map/while/body/eval_jaxpr/psum | solution.py:112
  1486.7 101.1 %copy-start.6 = (f32[2,64,4096]{2,1,0:T(8,128)S(1)}, f32[2,64,4096]{2,1,0:T(8,128)}, u32[]{:S(2)}) copy-start(f32[2,64,4096]{2,1,0:T(8,128)} %get-tuple-element.920) | copy-start | bytes 6291460 | tf_op jit(solution)/shard_map/while
  1592.7 4.8 collective-permute-start.1
  1597.4 109.2 %all-reduce.5.cloned.1.call-start = ((), (), s32[]{:S(2)}) async-start(), calls=%async_computation.3 | async-start | bytes 2097152 | tf_op jit(solution)/shard_map/while/body/eval_jaxpr/psum | solution.py:112
  1711.6 4.8 collective-permute-start.1
  1716.4 109.2 %all-reduce.5.cloned.1.call-start = ((), (), s32[]{:S(2)}) async-start(), calls=%async_computation.3 | async-start | bytes 2097152 | tf_op jit(solution)/shard_map/while/body/eval_jaxpr/psum | solution.py:112
  1724.5 101.1 %copy-start.6 = (f32[2,64,4096]{2,1,0:T(8,128)S(1)}, f32[2,64,4096]{2,1,0:T(8,128)}, u32[]{:S(2)}) copy-start(f32[2,64,4096]{2,1,0:T(8,128)} %get-tuple-element.920) | copy-start | bytes 6291460 | tf_op jit(solution)/shard_map/while
  1830.5 4.8 collective-permute-start.1
  1835.3 109.2 %all-reduce.5.cloned.1.call-start = ((), (), s32[]{:S(2)}) async-start(), calls=%async_computation.3 | async-start | bytes 2097152 | tf_op jit(solution)/shard_map/while/body/eval_jaxpr/psum | solution.py:112
  1949.5 4.8 collective-permute-start.1
  1954.2 109.2 %all-reduce.5.cloned.1.call-start = ((), (), s32[]{:S(2)}) async-start(), calls=%async_computation.3 | async-start | bytes 2097152 | tf_op jit(solution)/shard_map/while/body/eval_jaxpr/psum | solution.py:112
  2068.4 4.8 collective-permute-start.1
  2073.1 109.2 %all-reduce.5.cloned.1.call-start = ((), (), s32[]{:S(2)}) async-start(), calls=%async_computation.3 | async-start | bytes 2097152 | tf_op jit(solution)/shard_map/while/body/eval_jaxpr/psum | solution.py:112
  2187.3 4.8 collective-permute-start.1
  2192.1 109.2 %all-reduce.5.cloned.1.call-start = ((), (), s32[]{:S(2)}) async-start(), calls=%async_computation.3 | async-start | bytes 2097152 | tf_op jit(solution)/shard_map/while/body/eval_jaxpr/psum | solution.py:112
  2306.2 4.8 collective-permute-start.1
  (153 other events, 1570.5 us)
Sparse Core Ops, SparseCore 0:
  10.1 45.7 all-gather.2
  115.5 89.9 all-reduce.2
  228.5 99.1 all-reduce.2
  350.8 99.2 all-reduce.2
  473.1 99.2 all-reduce.2
  595.5 99.2 all-reduce.2
  717.9 99.2 all-reduce.2
  840.2 99.1 all-reduce.2
  962.5 99.2 all-reduce.2
  1084.8 99.1 all-reduce.2
  1194.5 55.0 all-gather.4
  1263.2 86.6 all-reduce.4
  1371.3 97.4 all-reduce.4
  1490.2 97.4 all-reduce.4
  1609.1 97.4 all-reduce.4
  1728.1 97.4 all-reduce.4
  1847.0 97.4 all-reduce.4
  1965.9 97.4 all-reduce.4
  2084.9 97.4 all-reduce.4
  2203.8 97.4 all-reduce.4
where the time goes:
time: 2330 us; the launch traced here: 2320 us
  waiting for transfers between devices  1820 us (78%)
  matrix products  183 us (8%)
  other arithmetic  143 us (6%)
  local copies, waits for them, and re-layouts  132 us (6%)
  starting transfers between devices  23.7 us (1%)
    psum x9, waiting for transfers between devices, forward_step_once(): summed = lax.psum(partial_out, 'tensor')  860 us
    psum x9, waiting for transfers between devices, backward_tick(): dnorm = lax.psum(partial_grad, 'tensor')  847 us
    dot_general x27, matrix products, contract_last(): lax.dot_general(left, right, (((1,), (1,)), ((), ())), preferred_element_...  103 us
    dynamic_update_slice x18, other arithmetic, retain_place(): lax.dynamic_update_index_in_dim(buffer, jnp.where(valid_flag, value, olde...  64.6 us
    dynamic_slice x27, local copies, waits for them, and re-layouts, retain_place(): older = lax.dynamic_index_in_dim(buffer, store_place, 0, keepdims=False)  62.6 us
    all_gather x1, waiting for transfers between devices, local(): lax.all_gather(out_grad, 'tensor', axis=1, tiled=True)  57.3 us
    ppermute x18, waiting for transfers between devices, shifted(): lax.ppermute(value, axis, [(source, source + steps) for source in range(f...  52.8 us
    dot_general x9, matrix products, forward_step_once(): upval = jnp.dot(normed, umat, preferred_element_type=jnp.float32)  47.3 us
  transfers between devices with their start and end apart: 38, of which 37 were waited for; matrix products, arithmetic and copies ran while one was open for 6% of the time, Pallas kernels for 0%

commit v1 on v0

v1 whole, which is shorter than its diff:
```python
import functools

import jax
import jax.numpy as jnp
from jax import lax
from jax.experimental import pallas as pl
from jax.experimental.pallas import tpu as pltpu
from jax.sharding import PartitionSpec as P

EPS = 1e-05
MB = 2
CHUNK = 256
BLOCK = 128
F32 = jnp.float32
BF16 = jnp.bfloat16
MESH = pl.DeviceIdType.MESH

STEP = (2, 1, 3, 0)
OFFSETS = [(a, b) for a in STEP for b in STEP]
NEGATED = [OFFSETS.index(((-a) % 4, (-b) % 4)) for a, b in OFFSETS]


def hops(k):
    return sum(min(d, 4 - d) for d in OFFSETS[k])


FAR_FIRST = sorted(range(16), key=lambda k: -hops(k))
SELF = 15


def step_of(u):
    return lax.rem(2 + 3 * u + 3 * (u * (u - 1) // 2), 4)


def kernel(
    x_ref, g_ref, gain_ref, mask_ref, gate_hbm, up_hbm, down_hbm,
    outf_hbm, outb_hbm,
    wgu, wd, wgu_t, wd_t, xin, cin, recv_f, recv_b, send_f, send_b, hsend, csend,
    ret_f, ret_b, pre, rows, xg, dgu, gain_in, gain_out,
    load_sem, xin_sem, cin_sem, rsf_sem, rsb_sem, retf_sem, retb_sem, send_sem, out_sem,
):
    me = lax.axis_index("pipe")
    my = lax.axis_index("tensor")
    my_a, my_b = my // 4, lax.rem(my, 4)
    rows_of = xin.shape[1]
    width = xin.shape[2]
    hidden = wd.shape[0]
    blocks = hidden // BLOCK
    last = 7

    def to(k):
        a, b = OFFSETS[k]
        return lax.rem(my_a + a, 4) * 4 + lax.rem(my_b + b, 4)

    def source(k):
        a, b = OFFSETS[k]
        return lax.rem(my_a + (4 - a), 4) * 4 + lax.rem(my_b + (4 - b), 4)

    def cols(k):
        return pl.ds(k * CHUNK, CHUNK)

    def lanes(c):
        return pl.ds(pl.multiple_of(c * CHUNK, CHUNK), CHUNK)

    def remote(src, dst, sent, got, stage, index):
        return pltpu.make_async_remote_copy(
            src_ref=src, dst_ref=dst, send_sem=sent, recv_sem=got,
            device_id=(stage, index), device_id_type=MESH,
        )

    loads = []
    for k in range(16):
        rows_hbm = lanes(source(k))
        loads.append(pltpu.make_async_copy(
            gate_hbm.at[0, rows_hbm, :], wgu.at[pl.ds(k * CHUNK, CHUNK), pl.ds(0, hidden)], load_sem.at[0, k]))
        loads.append(pltpu.make_async_copy(
            up_hbm.at[0, rows_hbm, :], wgu.at[pl.ds(k * CHUNK, CHUNK), pl.ds(hidden, hidden)], load_sem.at[1, k]))
    for k in range(16):
        loads.append(pltpu.make_async_copy(
            down_hbm.at[0, :, lanes(to(k))], wd.at[:, cols(k)], load_sem.at[2, k]))
    for copy in loads:
        copy.start()

    barrier = pltpu.get_barrier_semaphore()
    for k in range(15):
        pl.semaphore_signal(barrier, inc=1, device_id=(me, to(k)), device_id_type=MESH)

    @pl.when(me > 0)
    def _():
        for k in range(16):
            pl.semaphore_signal(barrier, inc=1, device_id=(me - 1, to(k)), device_id_type=MESH)

    @pl.when(me < last)
    def _():
        for k in range(16):
            pl.semaphore_signal(barrier, inc=1, device_id=(me + 1, to(k)), device_id_type=MESH)

    edge = (me == 0) | (me == last)

    @pl.when(edge)
    def _():
        pl.semaphore_wait(barrier, 31)

    @pl.when(jnp.logical_not(edge))
    def _():
        pl.semaphore_wait(barrier, 47)

    def gather(src_ref, dst, got, sent):
        for m in range(MB):
            src = src_ref.at[pl.ds(m * rows_of, rows_of), :]
            pltpu.make_async_copy(src, dst.at[m, :, cols(SELF)], got.at[m]).start()
            for k in FAR_FIRST[:15]:
                remote(src, dst.at[m, :, cols(k)], sent.at[m], got.at[m], me, to(k)).start()

    @pl.when(me == 0)
    def _():
        gather(x_ref, xin, xin_sem, send_sem.at[4])

    @pl.when(me == last)
    def _():
        gather(g_ref, cin, cin_sem, send_sem.at[4])

    for k in range(16):
        gain_in[:, k * CHUNK:(k + 1) * CHUNK] = gain_ref[:, lanes(source(k))]
        gain_out[:, k * CHUNK:(k + 1) * CHUNK] = gain_ref[:, lanes(to(k))]

    def keep(which, i, j):
        return jnp.full((BLOCK, BLOCK), mask_ref[0, which, i, j].astype(F32)).astype(BF16)

    @pl.loop(0, 16)
    def _(k):
        a, b = step_of(k // 4), step_of(lax.rem(k, 4))
        c = lax.rem(my_a + 4 - a, 4) * 4 + lax.rem(my_b + 4 - b, 4)
        at = pl.ds(pl.multiple_of(k * CHUNK, CHUNK), CHUNK)
        for which in range(2):
            piece = wgu.at[at, pl.ds(which * hidden, hidden)]
            pltpu.make_async_copy(piece, piece, load_sem.at[which, k]).wait()
        for half in range(2):
            r = pl.ds(pl.multiple_of(k * CHUNK + half * BLOCK, BLOCK), BLOCK)
            for which in range(2):
                for j in range(blocks):
                    o = which * hidden + j * BLOCK
                    wgu[r, o:o + BLOCK] = wgu[r, o:o + BLOCK] * keep(which, c * 2 + half, j)

    @pl.loop(0, 16)
    def _(k):
        a, b = step_of(k // 4), step_of(lax.rem(k, 4))
        c = lax.rem(my_a + a, 4) * 4 + lax.rem(my_b + b, 4)
        piece = wd.at[:, pl.ds(pl.multiple_of(k * CHUNK, CHUNK), CHUNK)]
        pltpu.make_async_copy(piece, piece, load_sem.at[2, k]).wait()
        for half in range(2):
            r = pl.ds(pl.multiple_of(k * CHUNK + half * BLOCK, BLOCK), BLOCK)
            for j in range(blocks):
                o = j * BLOCK
                wd[o:o + BLOCK, r] = wd[o:o + BLOCK, r] * keep(2, c * 2 + half, j)

    def transpose_weights():
        @pl.loop(0, 16)
        def _(k):
            u, v = k // 4, lax.rem(k, 4)
            nu, nv = lax.rem(u * 2, 3) + 3 * (u // 3), lax.rem(v * 2, 3) + 3 * (v // 3)
            n = nu * 4 + nv
            here = pl.ds(pl.multiple_of(k * CHUNK, CHUNK), CHUNK)
            there = pl.ds(pl.multiple_of(n * CHUNK, CHUNK), CHUNK)
            for j in range(2 * hidden // CHUNK):
                o = j * CHUNK
                wgu_t[o:o + CHUNK, there] = wgu[here, o:o + CHUNK].T
            for j in range(blocks):
                o = j * BLOCK
                wd_t[there, o:o + BLOCK] = wd[o:o + BLOCK, here].T

    @pl.when(me >= 4)
    def _():
        transpose_weights()

    def whole(ref, sem):
        pltpu.make_async_copy(ref, ref, sem).wait()

    def forward_compute(m):
        whole(xin.at[m], xin_sem.at[m])

        @pl.when(me > 0)
        def _():
            remote(xin.at[m], ret_f.at[m], send_sem.at[5, m], retf_sem.at[m], me - 1, my).start()

        square = jnp.zeros((rows_of, 1), F32)
        for k in range(16):
            part = xin[m, :, k * CHUNK:(k + 1) * CHUNK].astype(F32)
            square = square + jnp.sum(part * part, axis=1, keepdims=True)
            xg[:, k * CHUNK:(k + 1) * CHUNK] = (part * gain_in[:, k * CHUNK:(k + 1) * CHUNK]).astype(BF16)
        scale = lax.rsqrt(square * (1.0 / width) + EPS)
        rows[m] = jnp.broadcast_to(scale, (rows_of, BLOCK))
        both = jnp.dot(xg[...], wgu[...], preferred_element_type=F32) * scale
        pre[m] = both
        gate, up = both[:, :hidden], both[:, hidden:]
        act = (gate * jax.nn.sigmoid(gate) * up).astype(BF16)
        for n in range(2):
            o = n * 8 * CHUNK
            part = jnp.dot(act, wd[:, o:o + 8 * CHUNK], preferred_element_type=F32)
            for q in range(8):
                send_f[m, n * 8 + q] = part[:, q * CHUNK:(q + 1) * CHUNK].astype(BF16)
            for q in range(8):
                k = n * 8 + q
                if k != SELF:
                    remote(send_f.at[m, k], recv_f.at[m, k], send_sem.at[0, m], rsf_sem.at[m], me, to(k)).start()

    def total(recv, send, m, sem):
        whole(recv.at[m, pl.ds(0, 15)], sem.at[m])
        acc = send[m, SELF].astype(F32)
        for k in range(15):
            acc = acc + recv[m, k].astype(F32)
        return acc

    own = slice(SELF * CHUNK, (SELF + 1) * CHUNK)

    def forward_reduce(m):
        acc = total(recv_f, send_f, m, rsf_sem)
        hsend[m] = (xin[m, :, own].astype(F32) + acc).astype(BF16)

        @pl.when(me < last)
        def _():
            for k in FAR_FIRST:
                remote(hsend.at[m], xin.at[m, :, cols(k)], send_sem.at[1, m], xin_sem.at[m], me + 1, to(k)).start()

        @pl.when(me == last)
        def _():
            ret_f[m, :, own] = hsend[m]
            for k in FAR_FIRST[:15]:
                remote(hsend.at[m], ret_f.at[m, :, cols(k)], send_sem.at[1, m], retf_sem.at[m], me, to(k)).start()

    def backward_compute(m):
        whole(cin.at[m], cin_sem.at[m])

        @pl.when(me < last)
        def _():
            remote(cin.at[m], ret_b.at[m], send_sem.at[6, m], retb_sem.at[m], me + 1, my).start()

        dh = jnp.dot(cin[m], wd_t[...], preferred_element_type=F32)
        gate, up = pre[m, :, :hidden], pre[m, :, hidden:]
        sig = jax.nn.sigmoid(gate)
        dgate = (dh * up * sig * (1.0 + gate * (1.0 - sig))).astype(BF16)
        dup = (dh * gate * sig).astype(BF16)
        dgu[:, :hidden] = dgate
        dgu[:, hidden:] = dup
        inner = jnp.sum(dgate.astype(F32) * gate + dup.astype(F32) * up, axis=1, keepdims=True)
        scale = rows[m, :, 0:1]
        inner = inner * scale * scale * (1.0 / width)
        for n in range(4):
            o = n * 4 * CHUNK
            part = jnp.dot(dgu[...], wgu_t[:, o:o + 4 * CHUNK], preferred_element_type=F32)
            for q in range(4):
                k = n * 4 + q
                s = NEGATED[k]
                xval = xin[m, :, s * CHUNK:(s + 1) * CHUNK].astype(F32)
                back = part[:, q * CHUNK:(q + 1) * CHUNK] * gain_out[:, k * CHUNK:(k + 1) * CHUNK] * scale
                send_b[m, k] = (back - xval * inner).astype(BF16)
            for q in range(4):
                k = n * 4 + q
                if k != SELF:
                    remote(send_b.at[m, k], recv_b.at[m, k], send_sem.at[2, m], rsb_sem.at[m], me, to(k)).start()

    def backward_reduce(m):
        acc = total(recv_b, send_b, m, rsb_sem)
        csend[m] = (cin[m, :, own].astype(F32) + acc).astype(BF16)

        @pl.when(me > 0)
        def _():
            for k in FAR_FIRST:
                remote(csend.at[m], cin.at[m, :, cols(k)], send_sem.at[3, m], cin_sem.at[m], me - 1, to(k)).start()

        @pl.when(me == 0)
        def _():
            ret_b[m, :, own] = csend[m]
            for k in FAR_FIRST[:15]:
                remote(csend.at[m], ret_b.at[m, :, cols(k)], send_sem.at[3, m], retb_sem.at[m], me, to(k)).start()

    @pl.loop(0, MB + 1)
    def _(i):
        @pl.when(i < MB)
        def _():
            forward_compute(i)

        @pl.when((i > 0) & (me < last))
        def _():
            forward_reduce(i - 1)

    @pl.when(me < 4)
    def _():
        transpose_weights()

    @pl.loop(0, MB + 1)
    def _(i):
        @pl.when(i < MB)
        def _():
            backward_compute(i)

        @pl.when((i > 0) & (me == last))
        def _():
            forward_reduce(i - 1)

        @pl.when(i > 0)
        def _():
            backward_reduce(i - 1)

    def put(ret, sem, out_hbm, which, edge):
        @pl.loop(0, MB)
        def _(m):
            @pl.when(me == edge)
            def _():
                whole(ret.at[m, :, pl.ds(0, 15 * CHUNK)], sem.at[m])

            @pl.when(me != edge)
            def _():
                whole(ret.at[m], sem.at[m])

            for k in range(16):
                pltpu.make_async_copy(
                    ret.at[m, :, cols(k)],
                    out_hbm.at[0, pl.ds(pl.multiple_of(m * rows_of, 16), rows_of), lanes(source(k))],
                    out_sem.at[which, m],
                ).start()

    put(ret_f, retf_sem, outf_hbm, 0, last)
    put(ret_b, retb_sem, outb_hbm, 1, 0)

    @pl.loop(0, MB)
    def _(m):
        fifteen = recv_f.at[m, pl.ds(0, 15)]
        whole(fifteen, send_sem.at[0, m])
        whole(fifteen, send_sem.at[2, m])

        @pl.when(me < last)
        def _():
            whole(xin.at[m], send_sem.at[1, m])
            whole(xin.at[m], send_sem.at[6, m])

        @pl.when(me == last)
        def _():
            whole(fifteen, send_sem.at[1, m])

        @pl.when(me > 0)
        def _():
            whole(xin.at[m], send_sem.at[3, m])
            whole(xin.at[m], send_sem.at[5, m])

        @pl.when(me == 0)
        def _():
            whole(fifteen, send_sem.at[3, m])

        @pl.when((me == 0) | (me == last))
        def _():
            whole(fifteen, send_sem.at[4, m])

        whole(ret_f.at[m], out_sem.at[0, m])
        whole(ret_b.at[m], out_sem.at[1, m])


def local(inputs, out_grad, norm_gain, gate_weight, up_weight, down_weight, block_mask):
    count, chunk = inputs.shape
    width = norm_gain.shape[1]
    hidden = gate_weight.shape[2]
    r = count // MB
    vmem = pl.BlockSpec(memory_space=pltpu.VMEM)
    anyspace = pl.BlockSpec(memory_space=pl.ANY)
    dma = pltpu.SemaphoreType.DMA
    full = lambda dtype=BF16: pltpu.VMEM((MB, r, width), dtype)
    parts = lambda: pltpu.VMEM((MB, 16, r, chunk), BF16)
    forward, backward = pl.pallas_call(
        kernel,
        out_shape=[jax.ShapeDtypeStruct((1, count, width), BF16)] * 2,
        in_specs=[vmem, vmem, vmem, pl.BlockSpec(memory_space=pltpu.SMEM), anyspace, anyspace, anyspace],
        out_specs=[anyspace, anyspace],
        scratch_shapes=[
            pltpu.VMEM((width, 2 * hidden), BF16),
            pltpu.VMEM((hidden, width), BF16),
            pltpu.VMEM((2 * hidden, width), BF16),
            pltpu.VMEM((width, hidden), BF16),
            full(), full(),
            parts(), parts(), parts(), parts(),
            pltpu.VMEM((MB, r, chunk), BF16),
            pltpu.VMEM((MB, r, chunk), BF16),
            full(), full(),
            pltpu.VMEM((MB, r, 2 * hidden), F32),
            pltpu.VMEM((MB, r, BLOCK), F32),
            pltpu.VMEM((r, width), BF16),
            pltpu.VMEM((r, 2 * hidden), BF16),
            pltpu.VMEM((1, width), F32),
            pltpu.VMEM((1, width), F32),
            dma((3, 16)),
            dma((MB,)), dma((MB,)), dma((MB,)), dma((MB,)), dma((MB,)), dma((MB,)),
            dma((7, MB)),
            dma((2, MB)),
        ],
        compiler_params=pltpu.CompilerParams(
            collective_id=0, has_side_effects=True, vmem_limit_bytes=67043328
        ),
        name="window",
    )(inputs, out_grad, norm_gain, block_mask, gate_weight, up_weight, down_weight)
    return forward.astype(F32), backward.astype(F32)


def solution(mesh):
    in_specs = (
        P(None, "tensor"),
        P(None, "tensor"),
        P("pipe", None),
        P("pipe", None, "tensor"),
        P("pipe", None, "tensor"),
        P("pipe", "tensor", None),
        P("pipe", None, None, "tensor"),
    )
    out_specs = (P("pipe", None, None), P("pipe", None, None))
    return jax.shard_map(local, mesh=mesh, in_specs=in_specs, out_specs=out_specs, check_vma=False)
```

time: 2330 us -> 322 us (0.14)
  waiting for transfers between devices: 1820 us -> 0 us
  Pallas kernels: 0 us -> 314 us
  matrix products: 183 us -> 0 us
  other arithmetic: 143 us -> 5.51 us
  local copies, waits for them, and re-layouts: 132 us -> 1.42 us
  starting transfers between devices: 23.7 us -> 0 us
    psum x18 -> x0, waiting for transfers between devices: 1710 us -> none  [the longest x9 860 us: forward_step_once(): summed = lax.psum(partial_out, 'tensor')]
    pallas_call x0 -> x1, Pallas kernels: none -> 314 us  [local(): pl.pallas_call(kernel, out_shape=[jax.ShapeDtypeStruct((1, count, width),...]
    dot_general x54 -> x0, matrix products: 183 us -> none  [the longest x27 103 us: contract_last(): lax.dot_general(left, right, (((1,), (1,)), ((), ())), preferred_element_...]
    dynamic_update_slice x18 -> x0, other arithmetic: 64.6 us -> none  [retain_place(): lax.dynamic_update_index_in_dim(buffer, jnp.where(valid_flag, value, olde...]
    dynamic_slice x27 -> x0, local copies, waits for them, and re-layouts: 62.6 us -> none  [retain_place(): older = lax.dynamic_index_in_dim(buffer, store_place, 0, keepdims=False)]
    all_gather x2 -> x0, waiting for transfers between devices: 57.3 us -> none  [the longest x1 57.3 us: local(): lax.all_gather(out_grad, 'tensor', axis=1, tiled=True)]
    ppermute x18 -> x0, waiting for transfers between devices: 52.8 us -> none  [shifted(): lax.ppermute(value, axis, [(source, source + steps) for source in range(f...]
    mul x3 -> x0, other arithmetic: 31.8 us -> none  [masked_blocks(): shaped * mask.astype(weight.dtype)[:, None, :, None]]
  transfers between devices with their start and end apart: 38 -> 0, of which waited for: 37 -> 0; matrix products, arithmetic and copies ran while one was open for 6% -> 0% of each run, Pallas kernels for 0% -> 0%
where the time goes in v1:
time: 322 us
  Pallas kernels  314 us (98%)
  other arithmetic  5.51 us (2%)
    pallas_call x1, Pallas kernels, local(): pl.pallas_call(kernel, out_shape=[jax.ShapeDtypeStruct((1, count, width),...  314 us

profile of v1, /device:TPU:0, one launch (start us, length us, event | category | flops | bytes accessed | tf_op | source)
XLA Modules:
  0.0 321.5 jit_solution(11850766801411250656)
XLA Ops:
  0.6 1.4 copy.9.mask_ref
  2.0 313.9 %window.1 = (bf16[1,128,4096]{2,1,0:T(8,128)(2,1)}, bf16[1,128,4096]{2,1,0:T(8,128)(2,1)}) custom-call(bf16[128,256]{1,0:T(8,128)(2,1)} %x_ref.1, bf16[128,256]{1,0:T(8,128)(2,1)} %g_ref.1, f32[1,4096]{1,0:T(1,128)} %gain_ref.1, s32[1,3,32,7]{3,2,1,0:T(8,128)} %copy.9.mask_ref, bf16[1,4096,896]{2,1,0:T(8,128)(2,1)} %gate_hbm.1, ...), custom_call_target="tpu_custom_call" | custom-call | tf_op jit(solution)/shard_map/window/pallas_call | solution.py:368
  316.0 2.8 convert_element_type.6
  318.8 2.8 convert_element_type.7

commit v2 on v1

--- a/solution.py
+++ b/solution.py
@@ -8,28 +8,44 @@
 from jax.sharding import PartitionSpec as P
 
 EPS = 1e-05
-MB = 2
+MB = 4
 CHUNK = 256
 BLOCK = 128
 F32 = jnp.float32
 BF16 = jnp.bfloat16
 MESH = pl.DeviceIdType.MESH
 
-STEP = (2, 1, 3, 0)
-OFFSETS = [(a, b) for a in STEP for b in STEP]
+OFFSETS = [
+    (2, 2),
+    (2, 1), (2, 3), (1, 2), (3, 2),
+    (2, 0), (0, 2), (1, 1), (3, 3), (1, 3), (3, 1),
+    (1, 0), (3, 0), (0, 1), (0, 3),
+    (0, 0),
+]
 NEGATED = [OFFSETS.index(((-a) % 4, (-b) % 4)) for a, b in OFFSETS]
-
-
-def hops(k):
-    return sum(min(d, 4 - d) for d in OFFSETS[k])
-
-
-FAR_FIRST = sorted(range(16), key=lambda k: -hops(k))
+GROUPS = ((11, 16), (5, 11), (0, 5))
+FORWARD_AT = -1
+BACKWARD_AT = -1
+GROUP_OF = [next(g for g, (lo, hi) in enumerate(GROUPS) if lo <= k < hi) for k in range(16)]
+
+
+def packed(values):
+    word = sum(v << (2 * k) for k, v in enumerate(values))
+    return word - (1 << 32) if word >= 1 << 31 else word
+
+
+PACKED = (packed([a for a, b in OFFSETS]), packed([b for a, b in OFFSETS]))
 SELF = 15
-
-
-def step_of(u):
-    return lax.rem(2 + 3 * u + 3 * (u * (u - 1) // 2), 4)
+NEAR_FIRST = tuple(range(15))
+
+
+def offset_of(k):
+    return [lax.shift_right_logical(jnp.int32(word), 2 * k) & 3 for word in PACKED]
+
+
+def opposite(k):
+    paired = ((k >= 1) & (k <= 4)) | ((k >= 7) & (k <= 14))
+    return jnp.where(paired, k + 2 * lax.rem(k, 2) - 1, k)
 
 
 def kernel(
@@ -95,31 +111,6 @@
         for k in range(16):
             pl.semaphore_signal(barrier, inc=1, device_id=(me + 1, to(k)), device_id_type=MESH)
 
-    edge = (me == 0) | (me == last)
-
-    @pl.when(edge)
-    def _():
-        pl.semaphore_wait(barrier, 31)
-
-    @pl.when(jnp.logical_not(edge))
-    def _():
-        pl.semaphore_wait(barrier, 47)
-
-    def gather(src_ref, dst, got, sent):
-        for m in range(MB):
-            src = src_ref.at[pl.ds(m * rows_of, rows_of), :]
-            pltpu.make_async_copy(src, dst.at[m, :, cols(SELF)], got.at[m]).start()
-            for k in FAR_FIRST[:15]:
-                remote(src, dst.at[m, :, cols(k)], sent.at[m], got.at[m], me, to(k)).start()
-
-    @pl.when(me == 0)
-    def _():
-        gather(x_ref, xin, xin_sem, send_sem.at[4])
-
-    @pl.when(me == last)
-    def _():
-        gather(g_ref, cin, cin_sem, send_sem.at[4])
-
     for k in range(16):
         gain_in[:, k * CHUNK:(k + 1) * CHUNK] = gain_ref[:, lanes(source(k))]
         gain_out[:, k * CHUNK:(k + 1) * CHUNK] = gain_ref[:, lanes(to(k))]
@@ -129,7 +120,7 @@
 
     @pl.loop(0, 16)
     def _(k):
-        a, b = step_of(k // 4), step_of(lax.rem(k, 4))
+        a, b = offset_of(k)
         c = lax.rem(my_a + 4 - a, 4) * 4 + lax.rem(my_b + 4 - b, 4)
         at = pl.ds(pl.multiple_of(k * CHUNK, CHUNK), CHUNK)
         for which in range(2):
@@ -142,9 +133,34 @@
                     o = which * hidden + j * BLOCK
                     wgu[r, o:o + BLOCK] = wgu[r, o:o + BLOCK] * keep(which, c * 2 + half, j)
 
+    edge = (me == 0) | (me == last)
+
+    @pl.when(edge)
+    def _():
+        pl.semaphore_wait(barrier, 31)
+
+    @pl.when(jnp.logical_not(edge))
+    def _():
+        pl.semaphore_wait(barrier, 47)
+
+    def gather(src_ref, dst, got, sent):
+        for m in range(MB):
+            src = src_ref.at[pl.ds(m * rows_of, rows_of), :]
+            pltpu.make_async_copy(src, dst.at[m, :, cols(SELF)], got.at[m, GROUP_OF[SELF]]).start()
+            for k in NEAR_FIRST:
+                remote(src, dst.at[m, :, cols(k)], sent.at[m], got.at[m, GROUP_OF[k]], me, to(k)).start()
+
+    @pl.when(me == 0)
+    def _():
+        gather(x_ref, xin, xin_sem, send_sem.at[4])
+
+    @pl.when(me == last)
+    def _():
+        gather(g_ref, cin, cin_sem, send_sem.at[4])
+
     @pl.loop(0, 16)
     def _(k):
-        a, b = step_of(k // 4), step_of(lax.rem(k, 4))
+        a, b = offset_of(k)
         c = lax.rem(my_a + a, 4) * 4 + lax.rem(my_b + b, 4)
         piece = wd.at[:, pl.ds(pl.multiple_of(k * CHUNK, CHUNK), CHUNK)]
         pltpu.make_async_copy(piece, piece, load_sem.at[2, k]).wait()
@@ -157,9 +173,7 @@
     def transpose_weights():
         @pl.loop(0, 16)
         def _(k):
-            u, v = k // 4, lax.rem(k, 4)
-            nu, nv = lax.rem(u * 2, 3) + 3 * (u // 3), lax.rem(v * 2, 3) + 3 * (v // 3)
-            n = nu * 4 + nv
+            n = opposite(k)
             here = pl.ds(pl.multiple_of(k * CHUNK, CHUNK), CHUNK)
             there = pl.ds(pl.multiple_of(n * CHUNK, CHUNK), CHUNK)
             for j in range(2 * hidden // CHUNK):
@@ -176,31 +190,51 @@
     def whole(ref, sem):
         pltpu.make_async_copy(ref, ref, sem).wait()
 
+    def arrived(ref, m, g, sem):
+        lo, hi = GROUPS[g]
+        span = slice(lo * CHUNK, hi * CHUNK)
+        whole(ref.at[m, :, span], sem.at[m, g])
+        return span
+
     def forward_compute(m):
-        whole(xin.at[m], xin_sem.at[m])
+        if FORWARD_AT < 0:
+            @pl.when((m > 0) & (me < last))
+            def _():
+                forward_reduce(m - 1)
+
+        square = jnp.zeros((rows_of, CHUNK), F32)
+        for g, (lo, hi) in enumerate(GROUPS):
+            span = arrived(xin, m, g, xin_sem)
+            for k in range(lo, hi):
+                one = slice(k * CHUNK, (k + 1) * CHUNK)
+                part = xin[m, :, one].astype(F32)
+                square = square + part * part
+                xg[:, one] = (part * gain_in[:, one]).astype(BF16)
+            part = jnp.dot(xg[:, span], wgu[span, :], preferred_element_type=F32)
+            pre[m] = part if g == 0 else pre[m] + part
 
         @pl.when(me > 0)
         def _():
             remote(xin.at[m], ret_f.at[m], send_sem.at[5, m], retf_sem.at[m], me - 1, my).start()
 
-        square = jnp.zeros((rows_of, 1), F32)
-        for k in range(16):
-            part = xin[m, :, k * CHUNK:(k + 1) * CHUNK].astype(F32)
-            square = square + jnp.sum(part * part, axis=1, keepdims=True)
-            xg[:, k * CHUNK:(k + 1) * CHUNK] = (part * gain_in[:, k * CHUNK:(k + 1) * CHUNK]).astype(BF16)
-        scale = lax.rsqrt(square * (1.0 / width) + EPS)
+        scale = lax.rsqrt(jnp.sum(square, axis=1, keepdims=True) * (1.0 / width) + EPS)
         rows[m] = jnp.broadcast_to(scale, (rows_of, BLOCK))
-        both = jnp.dot(xg[...], wgu[...], preferred_element_type=F32) * scale
+        both = pre[m] * scale
         pre[m] = both
         gate, up = both[:, :hidden], both[:, hidden:]
         act = (gate * jax.nn.sigmoid(gate) * up).astype(BF16)
-        for n in range(2):
-            o = n * 8 * CHUNK
-            part = jnp.dot(act, wd[:, o:o + 8 * CHUNK], preferred_element_type=F32)
-            for q in range(8):
-                send_f[m, n * 8 + q] = part[:, q * CHUNK:(q + 1) * CHUNK].astype(BF16)
-            for q in range(8):
-                k = n * 8 + q
+        for n in range(4):
+            o = n * 4 * CHUNK
+            if n == FORWARD_AT:
+                @pl.when((m > 0) & (me < last))
+                def _():
+                    forward_reduce(m - 1)
+
+            part = jnp.dot(act, wd[:, o:o + 4 * CHUNK], preferred_element_type=F32)
+            for q in range(4):
+                send_f[m, n * 4 + q] = part[:, q * CHUNK:(q + 1) * CHUNK].astype(BF16)
+            for q in range(4):
+                k = n * 4 + q
                 if k != SELF:
                     remote(send_f.at[m, k], recv_f.at[m, k], send_sem.at[0, m], rsf_sem.at[m], me, to(k)).start()
 
@@ -219,23 +253,31 @@
 
         @pl.when(me < last)
         def _():
-            for k in FAR_FIRST:
-                remote(hsend.at[m], xin.at[m, :, cols(k)], send_sem.at[1, m], xin_sem.at[m], me + 1, to(k)).start()
+            for k in (*NEAR_FIRST, SELF):
+                remote(hsend.at[m], xin.at[m, :, cols(k)], send_sem.at[1, m], xin_sem.at[m, GROUP_OF[k]], me + 1, to(k)).start()
 
         @pl.when(me == last)
         def _():
             ret_f[m, :, own] = hsend[m]
-            for k in FAR_FIRST[:15]:
+            for k in NEAR_FIRST:
                 remote(hsend.at[m], ret_f.at[m, :, cols(k)], send_sem.at[1, m], retf_sem.at[m], me, to(k)).start()
 
     def backward_compute(m):
-        whole(cin.at[m], cin_sem.at[m])
+        if BACKWARD_AT < 0:
+            @pl.when(m > 0)
+            def _():
+                backward_reduce(m - 1)
+
+        dh = None
+        for g in range(len(GROUPS)):
+            span = arrived(cin, m, g, cin_sem)
+            part = jnp.dot(cin[m, :, span], wd_t[span, :], preferred_element_type=F32)
+            dh = part if dh is None else dh + part
 
         @pl.when(me < last)
         def _():
             remote(cin.at[m], ret_b.at[m], send_sem.at[6, m], retb_sem.at[m], me + 1, my).start()
 
-        dh = jnp.dot(cin[m], wd_t[...], preferred_element_type=F32)
         gate, up = pre[m, :, :hidden], pre[m, :, hidden:]
         sig = jax.nn.sigmoid(gate)
         dgate = (dh * up * sig * (1.0 + gate * (1.0 - sig))).astype(BF16)
@@ -247,6 +289,11 @@
         inner = inner * scale * scale * (1.0 / width)
         for n in range(4):
             o = n * 4 * CHUNK
+            if n == BACKWARD_AT:
+                @pl.when(m > 0)
+                def _():
+                    backward_reduce(m - 1)
+
             part = jnp.dot(dgu[...], wgu_t[:, o:o + 4 * CHUNK], preferred_element_type=F32)
             for q in range(4):
                 k = n * 4 + q
@@ -265,42 +312,46 @@
 
         @pl.when(me > 0)
         def _():
-            for k in FAR_FIRST:
-                remote(csend.at[m], cin.at[m, :, cols(k)], send_sem.at[3, m], cin_sem.at[m], me - 1, to(k)).start()
+            for k in (*NEAR_FIRST, SELF):
+                remote(csend.at[m], cin.at[m, :, cols(k)], send_sem.at[3, m], cin_sem.at[m, GROUP_OF[k]], me - 1, to(k)).start()
 
         @pl.when(me == 0)
         def _():
             ret_b[m, :, own] = csend[m]
-            for k in FAR_FIRST[:15]:
+            for k in NEAR_FIRST:
                 remote(csend.at[m], ret_b.at[m, :, cols(k)], send_sem.at[3, m], retb_sem.at[m], me, to(k)).start()
 
-    @pl.loop(0, MB + 1)
+    turn = jnp.where(me == last, 0, MB + 1)
+
+    @pl.loop(0, 2 * MB + 2)
     def _(i):
+        back = i - turn
+
         @pl.when(i < MB)
         def _():
             forward_compute(i)
 
-        @pl.when((i > 0) & (me < last))
-        def _():
-            forward_reduce(i - 1)
-
-    @pl.when(me < 4)
-    def _():
-        transpose_weights()
-
-    @pl.loop(0, MB + 1)
-    def _(i):
-        @pl.when(i < MB)
-        def _():
-            backward_compute(i)
-
-        @pl.when((i > 0) & (me == last))
-        def _():
-            forward_reduce(i - 1)
-
-        @pl.when(i > 0)
-        def _():
-            backward_reduce(i - 1)
+        @pl.when((i == MB) & (me < last))
+        def _():
+            forward_reduce(MB - 1)
+
+        @pl.when((i == MB) & (me < 4))
+        def _():
+            transpose_weights()
+
+        @pl.when((back >= 0) & (back < MB))
+        def _():
+            backward_compute(back)
+
+        @pl.when(back == MB)
+        def _():
+            backward_reduce(MB - 1)
+
+    @pl.when(me == last)
+    def _():
+        @pl.loop(0, MB)
+        def _(m):
+            forward_reduce(m)
 
     def put(ret, sem, out_hbm, which, edge):
         @pl.loop(0, MB)
@@ -387,7 +438,7 @@
             pltpu.VMEM((1, width), F32),
             pltpu.VMEM((1, width), F32),
             dma((3, 16)),
-            dma((MB,)), dma((MB,)), dma((MB,)), dma((MB,)), dma((MB,)), dma((MB,)),
+            dma((MB, len(GROUPS))), dma((MB, len(GROUPS))), dma((MB,)), dma((MB,)), dma((MB,)), dma((MB,)),
             dma((7, MB)),
             dma((2, MB)),
         ],

time: 322 us -> 274 us (0.85)
  Pallas kernels: 314 us -> 266 us
    pallas_call x1, Pallas kernels: 314 us -> 266 us  [local(): pl.pallas_call(kernel, out_shape=[jax.ShapeDtypeStruct((1, count, width),...]
where the time goes in v2:
time: 274 us
  Pallas kernels  266 us (97%)
  other arithmetic  5.51 us (2%)
    pallas_call x1, Pallas kernels, local(): pl.pallas_call(kernel, out_shape=[jax.ShapeDtypeStruct((1, count, width),...  266 us
    convert_element_type x2, other arithmetic, local(): return (forward.astype(F32), backward.astype(F32))  5.51 us

profile of v2, /device:TPU:0, one launch (start us, length us, event | category | flops | bytes accessed | tf_op | source)
XLA Modules:
  0.0 273.6 jit_solution(40457583400548113)
XLA Ops:
  0.6 1.4 copy.9.mask_ref
  2.0 266.0 %window.1 = (bf16[1,128,4096]{2,1,0:T(8,128)(2,1)}, bf16[1,128,4096]{2,1,0:T(8,128)(2,1)}) custom-call(bf16[128,256]{1,0:T(8,128)(2,1)} %x_ref.1, bf16[128,256]{1,0:T(8,128)(2,1)} %g_ref.1, f32[1,4096]{1,0:T(1,128)} %gain_ref.1, s32[1,3,32,7]{3,2,1,0:T(8,128)} %copy.9.mask_ref, bf16[1,4096,896]{2,1,0:T(8,128)(2,1)} %gate_hbm.1, ...), custom_call_target="tpu_custom_call" | custom-call | tf_op jit(solution)/shard_map/window/pallas_call | solution.py:419
  268.1 2.8 %convert_element_type.6 = f32[1,128,4096]{2,1,0:T(8,128)} convert(bf16[1,128,4096]{2,1,0:T(8,128)(2,1)} %get-tuple-element.4) | non-fusion elementwise | flops 524288 | bytes 3145728 | tf_op jit(solution)/shard_map/convert_element_type | solution.py:450
  270.8 2.8 %convert_element_type.7 = f32[1,128,4096]{2,1,0:T(8,128)} convert(bf16[1,128,4096]{2,1,0:T(8,128)(2,1)} %get-tuple-element.5) | non-fusion elementwise | flops 524288 | bytes 3145728 | tf_op jit(solution)/shard_map/convert_element_type | solution.py:450

commit v3 on v2

--- a/solution.py
+++ b/solution.py
@@ -9,6 +9,7 @@
 
 EPS = 1e-05
 MB = 4
+PIECES = 4
 CHUNK = 256
 BLOCK = 128
 F32 = jnp.float32
@@ -264,7 +265,7 @@
 
     def backward_compute(m):
         if BACKWARD_AT < 0:
-            @pl.when(m > 0)
+            @pl.when((m > 0) & (m < MB - 1))
             def _():
                 backward_reduce(m - 1)
 
@@ -345,7 +346,8 @@
 
         @pl.when(back == MB)
         def _():
-            backward_reduce(MB - 1)
+            for m in (MB - 2, MB - 1):
+                backward_reduce(m)
 
     @pl.when(me == last)
     def _():
@@ -404,6 +406,23 @@
 
         whole(ret_f.at[m], out_sem.at[0, m])
         whole(ret_b.at[m], out_sem.at[1, m])
+
+
+def widen(f_hbm, b_hbm, fo_hbm, bo_hbm, narrow, wide, got, put):
+    r = narrow.shape[1] // PIECES
+    order = [(a, p) for p in range(PIECES) for a in range(2)]
+    src, dst = (f_hbm, b_hbm), (fo_hbm, bo_hbm)
+    rows = lambda p: pl.ds(p * r, r)
+    ins = [pltpu.make_async_copy(src[a].at[0, rows(p), :], narrow.at[a, rows(p), :], got.at[a, p]) for a, p in order]
+    outs = [pltpu.make_async_copy(wide.at[a, rows(p), :], dst[a].at[0, rows(p), :], put.at[a, p]) for a, p in order]
+    for copy in ins:
+        copy.start()
+    for (a, p), came, leaves in zip(order, ins, outs):
+        came.wait()
+        wide[a, p * r:(p + 1) * r, :] = narrow[a, p * r:(p + 1) * r, :].astype(F32)
+        leaves.start()
+    for copy in outs:
+        copy.wait()
 
 
 def local(inputs, out_grad, norm_gain, gate_weight, up_weight, down_weight, block_mask):
@@ -447,7 +466,19 @@
         ),
         name="window",
     )(inputs, out_grad, norm_gain, block_mask, gate_weight, up_weight, down_weight)
-    return forward.astype(F32), backward.astype(F32)
+    return pl.pallas_call(
+        widen,
+        out_shape=[jax.ShapeDtypeStruct((1, count, width), F32)] * 2,
+        in_specs=[anyspace] * 2,
+        out_specs=[anyspace] * 2,
+        scratch_shapes=[
+            pltpu.VMEM((2, count, width), BF16),
+            pltpu.VMEM((2, count, width), F32),
+            dma((2, PIECES)), dma((2, PIECES)),
+        ],
+        compiler_params=pltpu.CompilerParams(vmem_limit_bytes=16 * 1024 * 1024),
+        name="widen",
+    )(forward, backward)
 
 
 def solution(mesh):

time: 274 us -> 272 us (level)
  other arithmetic: 5.51 us -> 0 us
    convert_element_type x2 -> x0, other arithmetic: 5.51 us -> none  [local(): return (forward.astype(F32), backward.astype(F32))]
where the time goes in v3:
time: 272 us
  Pallas kernels  268 us (99%)
  local copies, waits for them, and re-layouts  3.86 us (1%)
    pallas_call x1, Pallas kernels, local(): pl.pallas_call(kernel, out_shape=[jax.ShapeDtypeStruct((1, count, width),...  265 us

profile of v3, /device:TPU:0, one launch (start us, length us, event | category | flops | bytes accessed | tf_op | source)
XLA Modules:
  0.0 272.1 jit_solution(9434969266951443331)
XLA Ops:
  0.6 1.4 copy.9.mask_ref
  2.0 265.2 %window.1 = (bf16[1,128,4096]{2,1,0:T(8,128)(2,1)}, bf16[1,128,4096]{2,1,0:T(8,128)(2,1)}) custom-call(bf16[128,256]{1,0:T(8,128)(2,1)} %x_ref.1, bf16[128,256]{1,0:T(8,128)(2,1)} %g_ref.1, f32[1,4096]{1,0:T(1,128)} %gain_ref.1, s32[1,3,32,7]{3,2,1,0:T(8,128)} %copy.9.mask_ref, bf16[1,4096,896]{2,1,0:T(8,128)(2,1)} %gate_hbm.1, ...), custom_call_target="tpu_custom_call" | custom-call | tf_op jit(solution)/shard_map/window/pallas_call | solution.py:438
  267.3 0.0 copy-start
  267.3 1.2 copy-done
  268.5 0.0 copy-start.1
  268.5 1.2 copy-done.1
  269.7 2.3 widen.1
Async XLA Ops:
  267.3 1.2 copy-start
  268.5 1.2 copy-start.1

commit v4 on v3

--- a/solution.py
+++ b/solution.py
@@ -37,7 +37,7 @@
 
 PACKED = (packed([a for a, b in OFFSETS]), packed([b for a, b in OFFSETS]))
 SELF = 15
-NEAR_FIRST = tuple(range(15))
+SEND_ORDER = (0, 6, 3, 4, 13, 14, 1, 2, 7, 8, 9, 10, 5, 11, 12)
 
 
 def offset_of(k):
@@ -148,7 +148,7 @@
         for m in range(MB):
             src = src_ref.at[pl.ds(m * rows_of, rows_of), :]
             pltpu.make_async_copy(src, dst.at[m, :, cols(SELF)], got.at[m, GROUP_OF[SELF]]).start()
-            for k in NEAR_FIRST:
+            for k in SEND_ORDER:
                 remote(src, dst.at[m, :, cols(k)], sent.at[m], got.at[m, GROUP_OF[k]], me, to(k)).start()
 
     @pl.when(me == 0)
@@ -254,13 +254,13 @@
 
         @pl.when(me < last)
         def _():
-            for k in (*NEAR_FIRST, SELF):
+            for k in (*SEND_ORDER, SELF):
                 remote(hsend.at[m], xin.at[m, :, cols(k)], send_sem.at[1, m], xin_sem.at[m, GROUP_OF[k]], me + 1, to(k)).start()
 
         @pl.when(me == last)
         def _():
             ret_f[m, :, own] = hsend[m]
-            for k in NEAR_FIRST:
+            for k in SEND_ORDER:
                 remote(hsend.at[m], ret_f.at[m, :, cols(k)], send_sem.at[1, m], retf_sem.at[m], me, to(k)).start()
 
     def backward_compute(m):
@@ -313,13 +313,13 @@
 
         @pl.when(me > 0)
         def _():
-            for k in (*NEAR_FIRST, SELF):
+            for k in (*SEND_ORDER, SELF):
                 remote(csend.at[m], cin.at[m, :, cols(k)], send_sem.at[3, m], cin_sem.at[m, GROUP_OF[k]], me - 1, to(k)).start()
 
         @pl.when(me == 0)
         def _():
             ret_b[m, :, own] = csend[m]
-            for k in NEAR_FIRST:
+            for k in SEND_ORDER:
                 remote(csend.at[m], ret_b.at[m, :, cols(k)], send_sem.at[3, m], retb_sem.at[m], me, to(k)).start()
 
     turn = jnp.where(me == last, 0, MB + 1)

time: 272 us -> 271 us (level)
  no operation moved by 1% of the time
where the time goes in v4:
time: 271 us; the launch traced here: 270 us
  Pallas kernels  266 us (98%)
  local copies, waits for them, and re-layouts  3.86 us (1%)
    pallas_call x1, Pallas kernels, local(): pl.pallas_call(kernel, out_shape=[jax.ShapeDtypeStruct((1, count, width),...  264 us

profile of v4, /device:TPU:0, one launch (start us, length us, event | category | flops | bytes accessed | tf_op | source)
XLA Modules:
  0.0 270.4 jit_solution(10268736037522832609)
XLA Ops:
  0.6 1.4 copy.9.mask_ref
  2.0 263.6 %window.1 = (bf16[1,128,4096]{2,1,0:T(8,128)(2,1)}, bf16[1,128,4096]{2,1,0:T(8,128)(2,1)}) custom-call(bf16[128,256]{1,0:T(8,128)(2,1)} %x_ref.1, bf16[128,256]{1,0:T(8,128)(2,1)} %g_ref.1, f32[1,4096]{1,0:T(1,128)} %gain_ref.1, s32[1,3,32,7]{3,2,1,0:T(8,128)} %copy.9.mask_ref, bf16[1,4096,896]{2,1,0:T(8,128)(2,1)} %gate_hbm.1, ...), custom_call_target="tpu_custom_call" | custom-call | tf_op jit(solution)/shard_map/window/pallas_call | solution.py:438
  265.6 0.0 copy-start
  265.6 1.2 copy-done
  266.8 0.0 copy-start.1
  266.8 1.2 copy-done.1
  268.1 2.3 widen.1
Async XLA Ops:
  265.6 1.2 copy-start
  266.8 1.2 copy-start.1
